TPU v7x, 32 devices: a whole 2x2x4 slice. The times are simulated.
32 devices in a mesh: groups: 2 (over x), blk: 16 (over z, y, core).
Axes of the slice: x: 2, y: 2, z: 4, core: 2. Of those that a mesh axis runs over, the one named last changes fastest.
Arguments:
- frames: bfloat16 [256, 16384], P(('groups', 'blk')), parts along dimension 0
- basis: bfloat16 [256, 64], P(('groups', 'blk')), parts along dimension 0, may hold values from -6 to 6
- density: bfloat16 [256], P(('groups', 'blk')), parts along dimension 0, may hold values from 0.25 to 4
Outputs:
- residual_block: bfloat16 [256, 64], P(('groups', 'blk')), parts along dimension 0
- coefficients: float32 [128, 64], P('groups'), parts along dimension 0
There are 2 independent parts, one for each index of `groups`. A program takes and returns all parts, laid end to end along the dimension named above; each array names one. Nothing has to cross between parts.
All inputs are finite; a program needn't handle non-finite values.
Results may differ from a plain program's by a relative error of at most 0.0045.
Values may be sent and summed in bfloat16 or wider, within the bound.
No kernel may reach another device: no remote copies, remote signals or barrier semaphores. Data moves between devices by JAX's collectives and lax.ppermute only.
A program may use at most 64 MiB of HBM per device.

v0:
```python
import jax
import jax.numpy as jnp
from jax import lax
from jax.sharding import PartitionSpec as P


def pair_kernel(left, left_norms, right):
    right_norms = jnp.sum(jnp.square(right.astype(jnp.float32)), axis=1)
    inner_products = lax.dot_general(
        left, right, (((1,), (1,)), ((), ())), preferred_element_type=jnp.float32
    )
    squared_dist = left_norms[:, None] + right_norms[None, :] - 2.0 * inner_products
    return jnp.exp(-squared_dist / left.shape[1])


def shards(frames, basis, density):
    own_norms = jnp.sum(jnp.square(frames.astype(jnp.float32)), axis=1)
    row_count = frames.shape[0]
    blocks = lax.all_gather(frames, "blk", axis=0, tiled=True)
    vectors = lax.all_gather(basis, "blk", axis=0, tiled=True)
    weights_in = lax.all_gather(density, "blk", axis=0, tiled=True)
    kernel = pair_kernel(frames, own_norms, blocks)
    forward = (kernel * weights_in.astype(jnp.float32)[None, :]).astype(jnp.bfloat16)
    numer = jnp.dot(forward, vectors, preferred_element_type=jnp.float32)
    totals = jnp.sum(forward.astype(jnp.float32), axis=1)
    numer, totals = (numer, totals)
    applied = numer / totals[:, None]
    basis_f = basis.astype(jnp.float32)
    local_coef = lax.dot_general(
        basis_f,
        applied,
        (((0,), (0,)), ((), ())),
        precision=lax.Precision.HIGHEST,
        preferred_element_type=jnp.float32,
    )
    coefficients = lax.psum(local_coef, "blk")
    frame_total = row_count * lax.axis_size("blk")
    projection = jnp.dot(
        basis_f, coefficients, precision=lax.Precision.HIGHEST, preferred_element_type=jnp.float32
    )
    residual_block = (applied - projection / frame_total).astype(jnp.bfloat16)
    return (residual_block, coefficients)


def solution(mesh):
    placed = (P(("groups", "blk"), None), P(("groups", "blk"), None), P(("groups", "blk")))
    return jax.shard_map(
        shards,
        mesh=mesh,
        in_specs=placed,
        out_specs=(P(("groups", "blk"), None), P("groups", None)),
        check_vma=False,
    )
```

profile of v0, /device:TPU:0, one launch (start us, length us, event | category | flops | bytes accessed | tf_op | source)
XLA Modules:
  0.0 137.7 jit_solution(3754534518135585667)
XLA Ops:
  7.2 0.0 copy-start.1
  7.2 0.0 all-gather.2.cloned.1.call-start
  7.2 0.7 all-gather.2.cloned.1.call-update
  7.9 1.2 dynamic-slice
  9.8 0.9 dynamic-update-slice
  10.7 35.4 %all-reduce = bf16[128]{0:T(256)(128)(2,1)S(1)} all-reduce(bf16[128]{0:T(256)(128)(2,1)S(1)} %dynamic-update-slice), channel_id=1, replica_groups=mesh['groups'=2,'blk'=16] {'blk'}, use_global_device_ids=true, to_apply=%add | all-reduce | flops 128 | bytes 512
  46.1 17.6 %all_gather.11 = bf16[128,64]{1,0:T(8,128)(2,1)S(1)} all-gather(bf16[8,64]{1,0:T(8,128)(2,1)} %param.4), channel_id=1, replica_groups=mesh['groups'=2,'blk'=16] {'blk'}, dimensions={0}, use_global_device_ids=true | all-gather | bytes 17408 | tf_op jit(solution)/shard_map/all_gather | solution.py:20
  63.7 1.2 multiply_reduce_fusion.1
  64.9 0.0 all-gather.2.cloned.1.call-done
  64.9 0.0 copy-start
  64.9 0.0 copy-start.2
  64.9 3.2 %multiply_reduce_fusion = f32[128]{0:T(128)S(1)} fusion(bf16[128,16384]{1,0:T(8,128)(2,1)} %all-gather.2.cloned.1.call-done), kind=kLoop, calls=%fused_computation | loop fusion | flops 6291328 | bytes 4194816 | tf_op jit(solution)/shard_map/reduce_sum | solution.py:8
  68.2 0.0 copy-done.1
  68.2 0.2 copy-done
  68.4 1.3 convert_reduce_fusion
  69.7 0.1 convolution_divide_fusion
  69.8 0.0 copy-done.2
  69.8 0.2 convolution_bitcast_fusion
  70.0 59.3 %psum.7 = f32[64,64]{0,1:T(8,128)S(1)} all-reduce(f32[64,64]{0,1:T(8,128)S(1)} %convolution_bitcast_fusion), channel_id=1, replica_groups=mesh['groups'=2,'blk'=16] {'blk'}, use_global_device_ids=true, to_apply=%region_3.0 | all-reduce | flops 4096 | bytes 32768 | tf_op jit(solution)/shard_map/psum | solution.py:36
  129.4 0.7 fusion.8
  130.1 0.7 copy.5
  (2 shorter events, 0.0 us)
Async XLA Ops:
  7.2 61.0 %copy-start.1 = (bf16[8,16384]{1,0:T(8,128)(2,1)S(1)}, bf16[8,16384]{1,0:T(8,128)(2,1)}, u32[]{:S(2)}) copy-start(bf16[8,16384]{1,0:T(8,128)(2,1)} %param.3) | copy-start | bytes 786436
  7.2 57.7 %all-gather.2.cloned.1.call-start = ((), (), s32[]{:S(2)}) async-start(), calls=%async_computation | async-start | bytes 4456448 | tf_op jit(solution)/shard_map/all_gather | solution.py:19
  64.9 3.5 %copy-start = (bf16[128,16384]{1,0:T(8,128)(2,1)S(1)}, bf16[128,16384]{1,0:T(8,128)(2,1)}, u32[]{:S(2)}) copy-start(bf16[128,16384]{1,0:T(8,128)(2,1)} %all-gather.2.cloned.1.call-done) | copy-start | bytes 12582916
  64.9 4.9 %copy-start.2 = (bf16[8,64]{1,0:T(8,128)(2,1)S(1)}, bf16[8,64]{1,0:T(8,128)(2,1)}, u32[]{:S(2)}) copy-start(bf16[8,64]{1,0:T(8,128)(2,1)} %param.4) | copy-start | bytes 3076
Sparse Core Ops, SparseCore 0:
  10.2 53.5 all-gather.1
where the time goes:
time: 138 us
  blocking collectives  112 us (81%)
  between operations  14.7 us (11%)
  other arithmetic  4.43 us (3%)
  local copies, waits for them, and re-layouts  3.01 us (2%)
  matrix products  2.4 us (2%)
    psum x1, blocking collectives, shards(): coefficients = lax.psum(local_coef, 'blk')  59.3 us
    unnamed x1, blocking collectives  35.4 us
    all_gather x1, blocking collectives, shards(): vectors = lax.all_gather(basis, 'blk', axis=0, tiled=True)  17.6 us
    reduce_sum x1, other arithmetic, pair_kernel(): right_norms = jnp.sum(jnp.square(right.astype(jnp.float32)), axis=1)  3.23 us
    unnamed x10, local copies, waits for them, and re-layouts  3.01 us
  transfers between devices with their start and end apart: 1, of which 0 were waited for; matrix products, arithmetic and copies ran while one was open for 2% of the time, Pallas kernels for 0%

commit v1 on v0

--- a/solution.py
+++ b/solution.py
@@ -2,6 +2,18 @@
 import jax.numpy as jnp
 from jax import lax
 from jax.sharding import PartitionSpec as P
+
+
+def detail_quotas_now(t0):
+    n_shards = lax.axis_size("blk")
+    wide_out, piece_out = (t0, 0)
+    while 1 << piece_out < n_shards:
+        part_now = lax.ppermute(
+            wide_out, "blk", [(idx, idx ^ 1 << piece_out) for idx in range(n_shards)]
+        )
+        wide_out = wide_out + part_now
+        piece_out = piece_out + 1
+    return wide_out
 
 
 def pair_kernel(left, left_norms, right):
@@ -33,7 +45,7 @@
         precision=lax.Precision.HIGHEST,
         preferred_element_type=jnp.float32,
     )
-    coefficients = lax.psum(local_coef, "blk")
+    coefficients = detail_quotas_now(local_coef)
     frame_total = row_count * lax.axis_size("blk")
     projection = jnp.dot(
         basis_f, coefficients, precision=lax.Precision.HIGHEST, preferred_element_type=jnp.float32

time: 138 us -> 92.6 us (0.67)
  blocking collectives: 112 us -> 53 us
  waiting for transfers between devices: 0.69 us -> 11.3 us
  starting transfers between devices: 0.04 us -> 3.47 us
    psum x1 -> x0, blocking collectives: 59.3 us -> none  [shards(): coefficients = lax.psum(local_coef, 'blk')]
    ppermute x0 -> x4, waiting for transfers between devices: none -> 10.6 us  [detail_quotas_now(): lax.ppermute(wide_out, 'blk', [(idx, idx ^ 1 << piece_out) for idx in ran...]
    ppermute x0 -> x4, starting transfers between devices: none -> 3.43 us  [detail_quotas_now(): lax.ppermute(wide_out, 'blk', [(idx, idx ^ 1 << piece_out) for idx in ran...]
  transfers between devices with their start and end apart: 1 -> 5, of which waited for: 0 -> 4; matrix products, arithmetic and copies ran while one was open for 2% -> 4% of each run, Pallas kernels for 0% -> 0%
where the time goes in v1:
time: 92.6 us; the launch traced here: 92.4 us
  blocking collectives  53 us (57%)
  between operations  14.7 us (16%)
  waiting for transfers between devices  11.3 us (12%)
  other arithmetic  4.45 us (5%)
  starting transfers between devices  3.47 us (4%)
  local copies, waits for them, and re-layouts  3.01 us (3%)
  matrix products  2.4 us (3%)
    unnamed x1, blocking collectives  35.4 us
    all_gather x1, blocking collectives, shards(): vectors = lax.all_gather(basis, 'blk', axis=0, tiled=True)  17.6 us
    ppermute x4, waiting for transfers between devices, detail_quotas_now(): lax.ppermute(wide_out, 'blk', [(idx, idx ^ 1 << piece_out) for idx in ran...  10.6 us
    ppermute x4, starting transfers between devices, detail_quotas_now(): lax.ppermute(wide_out, 'blk', [(idx, idx ^ 1 << piece_out) for idx in ran...  3.43 us
    reduce_sum x1, other arithmetic, pair_kernel(): right_norms = jnp.sum(jnp.square(right.astype(jnp.float32)), axis=1)  3.23 us
    unnamed x10, local copies, waits for them, and re-layouts  3.01 us
  transfers between devices with their start and end apart: 5, of which 4 were waited for; matrix products, arithmetic and copies ran while one was open for 4% of the time, Pallas kernels for 0%

profile of v1, /device:TPU:0, one launch (start us, length us, event | category | flops | bytes accessed | tf_op | source)
XLA Modules:
  0.0 92.4 jit_solution(1895896976880183983)
XLA Ops:
  7.2 0.0 copy-start.1
  7.2 0.0 all-gather.2.cloned.1.call-start
  7.2 0.7 all-gather.2.cloned.1.call-update
  7.9 1.2 %dynamic-slice = u32[1]{0:T(128)} dynamic-slice(u32[32]{0:T(128)} %constant.15, u32[]{:T(128)S(6)} %add.32), dynamic_slice_sizes={1} | dynamic-slice | bytes 12
  9.8 0.9 dynamic-update-slice
  10.7 35.4 %all-reduce = bf16[128]{0:T(256)(128)(2,1)S(1)} all-reduce(bf16[128]{0:T(256)(128)(2,1)S(1)} %dynamic-update-slice), channel_id=1, replica_groups=mesh['groups'=2,'blk'=16] {'blk'}, use_global_device_ids=true, to_apply=%add | all-reduce | flops 128 | bytes 512
  46.1 17.6 %all_gather.11 = bf16[128,64]{1,0:T(8,128)(2,1)S(1)} all-gather(bf16[8,64]{1,0:T(8,128)(2,1)} %param.4), channel_id=1, replica_groups=mesh['groups'=2,'blk'=16] {'blk'}, dimensions={0}, use_global_device_ids=true | all-gather | bytes 17408 | tf_op jit(solution)/shard_map/all_gather | solution.py:32
  63.7 1.2 %multiply_reduce_fusion.1 = f32[8]{0:T(128)S(1)} fusion(bf16[8,16384]{1,0:T(8,128)(2,1)} %param.3), kind=kLoop, calls=%fused_computation.14 | loop fusion | flops 393208 | bytes 262176 | tf_op jit(solution)/shard_map/reduce_sum | solution.py:29
  64.9 0.0 all-gather.2.cloned.1.call-done
  64.9 0.0 copy-start
  64.9 0.0 copy-start.2
  64.9 3.2 %multiply_reduce_fusion = f32[128]{0:T(128)S(1)} fusion(bf16[128,16384]{1,0:T(8,128)(2,1)} %all-gather.2.cloned.1.call-done), kind=kLoop, calls=%fused_computation | loop fusion | flops 6291328 | bytes 4194816 | tf_op jit(solution)/shard_map/reduce_sum | solution.py:20
  68.2 0.0 copy-done.1
  68.2 0.2 copy-done
  68.4 1.3 %convert_reduce_fusion = (f32[8]{0:T(128)S(1)}, bf16[8,128]{1,0:T(8,128)(2,1)S(1)}) fusion(f32[128]{0:T(128)S(1)} %convert_element_type.21, bf16[8,16384]{1,0:T(8,128)(2,1)S(1)} %copy-done.1, bf16[128,16384]{1,0:T(8,128)(2,1)S(1)} %copy-done, f32[128]{0:T(128)S(1)} %multiply_reduce_fusion, f32[8]{0:T(128)S(1)} %multiply_reduce_fusion.1), kind=kOutput, calls=%fused_computation.15 | convolution fusion | flops 33563640 | bytes 4459584 | tf_op jit(solution)/shard_map/dot_general | solution.py:21
  69.7 0.1 convolution_divide_fusion
  69.8 0.0 copy-done.2
  69.8 0.2 convolution_bitcast_fusion
  70.0 0.4 collective-permute-start
  70.5 0.9 collective-permute-done
  71.3 2.0 %collective-permute-start.1 = (f32[64,64]{0,1:T(8,128)S(1)}, f32[64,64]{0,1:T(8,128)S(1)}, u32[]{:S(2)}, u32[]{:S(2)}) collective-permute-start(f32[64,64]{0,1:T(8,128)S(1)} %add.28), channel_id=1, source_target_pairs={{0,2},{1,3},{2,0},{3,1},{4,6},{5,7},{6,4},{7,5},{8,10},{9,11},{10,... | collective-permute-start | bytes 49160 | tf_op jit(solution)/shard_map/ppermute | solution.py:11
  73.3 1.9 %collective-permute-done.1 = f32[64,64]{0,1:T(8,128)S(1)} collective-permute-done((f32[64,64]{0,1:T(8,128)S(1)}, f32[64,64]{0,1:T(8,128)S(1)}, u32[]{:S(2)}, u32[]{:S(2)}) %collective-permute-start.1) | collective-permute-done | bytes 16416 | tf_op jit(solution)/shard_map/ppermute | solution.py:11
  75.2 0.4 collective-permute-start.2
  75.6 3.6 %collective-permute-done.2 = f32[64,64]{0,1:T(8,128)S(1)} collective-permute-done((f32[64,64]{0,1:T(8,128)S(1)}, f32[64,64]{0,1:T(8,128)S(1)}, u32[]{:S(2)}, u32[]{:S(2)}) %collective-permute-start.2) | collective-permute-done | bytes 16416 | tf_op jit(solution)/shard_map/ppermute | solution.py:11
  79.2 0.7 collective-permute-start.3
  79.8 4.3 %collective-permute-done.3 = f32[64,64]{0,1:T(8,128)S(1)} collective-permute-done((f32[64,64]{0,1:T(8,128)S(1)}, f32[64,64]{0,1:T(8,128)S(1)}, u32[]{:S(2)}, u32[]{:S(2)}) %collective-permute-start.3) | collective-permute-done | bytes 16416 | tf_op jit(solution)/shard_map/ppermute | solution.py:11
  84.1 0.7 fusion.8
  84.9 0.7 copy.5
  (6 shorter events, 0.0 us)
Async XLA Ops:
  7.2 61.0 %copy-start.1 = (bf16[8,16384]{1,0:T(8,128)(2,1)S(1)}, bf16[8,16384]{1,0:T(8,128)(2,1)}, u32[]{:S(2)}) copy-start(bf16[8,16384]{1,0:T(8,128)(2,1)} %param.3) | copy-start | bytes 786436
  7.2 57.7 %all-gather.2.cloned.1.call-start = ((), (), s32[]{:S(2)}) async-start(), calls=%async_computation | async-start | bytes 4456448 | tf_op jit(solution)/shard_map/all_gather | solution.py:31
  64.9 3.5 %copy-start = (bf16[128,16384]{1,0:T(8,128)(2,1)S(1)}, bf16[128,16384]{1,0:T(8,128)(2,1)}, u32[]{:S(2)}) copy-start(bf16[128,16384]{1,0:T(8,128)(2,1)} %all-gather.2.cloned.1.call-done) | copy-start | bytes 12582916
  64.9 4.9 %copy-start.2 = (bf16[8,64]{1,0:T(8,128)(2,1)S(1)}, bf16[8,64]{1,0:T(8,128)(2,1)}, u32[]{:S(2)}) copy-start(bf16[8,64]{1,0:T(8,128)(2,1)} %param.4) | copy-start | bytes 3076
  70.0 1.3 %collective-permute-start = (f32[64,64]{0,1:T(8,128)S(1)}, f32[64,64]{0,1:T(8,128)S(1)}, u32[]{:S(2)}, u32[]{:S(2)}) collective-permute-start(f32[64,64]{0,1:T(8,128)S(1)} %convolution_bitcast_fusion), channel_id=1, source_target_pairs={{0,1},{1,0},{2,3},{3,2},{4,5},{5,4},{6,7},{7,6},{8,9},{9,8},{10,11... | collective-permute-start | bytes 49160 | tf_op jit(solution)/shard_map/ppermute | solution.py:11
  71.3 3.9 %collective-permute-start.1 = (f32[64,64]{0,1:T(8,128)S(1)}, f32[64,64]{0,1:T(8,128)S(1)}, u32[]{:S(2)}, u32[]{:S(2)}) collective-permute-start(f32[64,64]{0,1:T(8,128)S(1)} %add.28), channel_id=1, source_target_pairs={{0,2},{1,3},{2,0},{3,1},{4,6},{5,7},{6,4},{7,5},{8,10},{9,11},{10,... | collective-permute-start | bytes 49160 | tf_op jit(solution)/shard_map/ppermute | solution.py:11
  75.2 3.9 %collective-permute-start.2 = (f32[64,64]{0,1:T(8,128)S(1)}, f32[64,64]{0,1:T(8,128)S(1)}, u32[]{:S(2)}, u32[]{:S(2)}) collective-permute-start(f32[64,64]{0,1:T(8,128)S(1)} %add.29), channel_id=1, source_target_pairs={{0,4},{1,5},{2,6},{3,7},{4,0},{5,1},{6,2},{7,3},{8,12},{9,13},{10,... | collective-permute-start | bytes 49160 | tf_op jit(solution)/shard_map/ppermute | solution.py:11
  79.2 5.0 %collective-permute-start.3 = (f32[64,64]{0,1:T(8,128)S(1)}, f32[64,64]{0,1:T(8,128)S(1)}, u32[]{:S(2)}, u32[]{:S(2)}) collective-permute-start(f32[64,64]{0,1:T(8,128)S(1)} %add.30), channel_id=1, source_target_pairs={{0,8},{1,9},{2,10},{3,11},{4,12},{5,13},{6,14},{7,15},{8,0},{9,1},... | collective-permute-start | bytes 49160 | tf_op jit(solution)/shard_map/ppermute | solution.py:11
Sparse Core Ops, SparseCore 0:
  10.2 53.5 all-gather.1
